TPU v7x, 256 devices: a whole 4x4x8 slice. The times are simulated.
256 devices in a mesh: sector: 8 (over y, core), inner: 32 (over x, z).
Axes of the slice: x: 4, y: 4, z: 8, core: 2. Of those that a mesh axis runs over, the one named last changes fastest.
Arguments:
- density: float32 [128, 64, 16384], P('inner', None, 'sector'), may hold values from -6 to 6
- source_sector: int32 [32, 8, 16], P('inner'), may hold values from 0 to 7, as said below
- source_tile: int32 [32, 8, 16], P('inner'), may hold values from 0 to 15
- matrix_id: int32 [32, 8, 16], P('inner'), may hold values from 0 to 31
- cubic_weights: float32 [32, 128, 128], replicated, may hold values from -0.6 to 1.5, as said below
- bin_cells: int32 [8, 32], P('sector'), may hold values from 1 to 128, 2048 in all within a row
- wave_level: float32 [8, 32], P('sector'), may hold values from 0.15 to 1
- energy_rate: float32 [128, 64], replicated, may hold values from 0.01 to 0.12
- pitch_rate: float32 [128, 64], replicated, may hold values from 0.01 to 0.12
Outputs:
- advanced: float32 [128, 64, 16384], P('inner', None, 'sector')
Inputs may be any that keep to these rules, and one draw needn't show every extreme that they name: `source_sector`: for every energy block and destination sector, at most 3 of its 16 tiles depart from any one sector, exactly 3 depart from one sector, and that sector lies one to three sectors below the destination, cyclically. `cubic_weights`: every row of every matrix sums to one.
All inputs are finite; a program needn't handle non-finite values.
Results may differ from a plain program's by a relative error of at most 0.000096.
Values sent between devices are 32-bit elements; how exact they have to be, the bound alone decides.
A program may use at most 128 MiB of HBM per device.

v0:
```python
import jax
import jax.numpy as jnp
from jax import lax
from jax.sharding import PartitionSpec as P

PASSES = 12


def order_within(sources):
    tile_count = sources.shape[1]
    same = sources[:, :, None] == sources[:, None, :]
    earlier = jnp.arange(tile_count)[None, :] < jnp.arange(tile_count)[:, None]
    return jnp.sum((same & earlier[None]).astype(jnp.int32), axis=2)


def drift_step(density, source_sector, source_tile, matrix_id, cubic_weights):
    sectors = lax.axis_size("sector")
    sector_here = lax.axis_index("sector")
    energies, pitches, cell_count = density.shape
    tile_len = cubic_weights.shape[1]
    tile_count = cell_count // tile_len
    slot_count = max(2, (3 * tile_count + 2 * sectors - 1) // (2 * sectors))
    sources = source_sector[0]
    picked_tiles = source_tile[0]
    matrix_ids = matrix_id[0]
    tile_ranks = order_within(sources)
    slot_rank = jnp.arange(slot_count, dtype=jnp.int32)
    matched = (sources[:, None, :] == sector_here) & (
        tile_ranks[:, None, :] == slot_rank[None, :, None]
    )
    chosen = jnp.sum(jnp.where(matched, picked_tiles[:, None, :], 0), axis=2).reshape(-1)
    filled = jnp.any(matched, axis=2).reshape(-1).astype(jnp.float32)
    blocks = density.reshape(energies, pitches, tile_count, tile_len)
    outgoing = jnp.take(blocks, chosen, axis=2) * filled[None, None, :, None]
    incoming = lax.all_to_all(outgoing, "sector", split_axis=2, concat_axis=2, tiled=True)
    own_sources = sources[sector_here]
    own_ranks = tile_ranks[sector_here]
    own_ids = matrix_ids[sector_here]
    where_from = own_sources * slot_count + own_ranks
    departing = jnp.take(incoming, where_from, axis=2)
    matrices = jnp.take(cubic_weights, own_ids, axis=0)
    drifted = jnp.einsum("eptj,tij->epti", departing, matrices, precision=lax.Precision.HIGHEST)
    return drifted.reshape(energies, pitches, cell_count)


def one_pass(field, rate_cell, energy_rate, pitch_rate):
    flux_e = energy_rate[:-1, :, None] * (field[1:] - field[:-1])
    flux_p = pitch_rate[:, :-1, None] * (field[:, 1:] - field[:, :-1])
    change_e = jnp.pad(flux_e, ((0, 1), (0, 0), (0, 0))) - jnp.pad(flux_e, ((1, 0), (0, 0), (0, 0)))
    change_p = jnp.pad(flux_p, ((0, 0), (0, 1), (0, 0))) - jnp.pad(flux_p, ((0, 0), (1, 0), (0, 0)))
    return field + rate_cell[None, None, :] * (change_e + change_p)


def shards(
    density,
    source_sector,
    source_tile,
    matrix_id,
    cubic_weights,
    bin_cells,
    wave_level,
    energy_rate,
    pitch_rate,
):
    first = drift_step(density, source_sector, source_tile, matrix_id, cubic_weights)
    inner_count = lax.axis_size("inner")
    inner_here = lax.axis_index("inner")
    cell_count = first.shape[2]
    lengths = bin_cells[0]
    per_device = cell_count // inner_count
    owner_cells = jnp.full((inner_count,), per_device, jnp.int32)
    owner_ends = jnp.cumsum(owner_cells)
    owner_starts = owner_ends - owner_cells
    offsets = jnp.arange(per_device, dtype=jnp.int32)
    cell_index = owner_starts[:, None] + offsets[None, :]
    valid = (offsets[None, :] < owner_cells[:, None]).reshape(-1).astype(jnp.float32)
    clipped = jnp.minimum(cell_index, cell_count - 1).reshape(-1)
    packed = jnp.take(first, clipped, axis=2) * valid[None, None, :]
    cellwise = lax.all_to_all(packed, "inner", split_axis=2, concat_axis=0, tiled=True)
    bin_ends = jnp.cumsum(lengths)
    global_cells = owner_starts[inner_here] + offsets
    is_live = (offsets < owner_cells[inner_here]).astype(jnp.float32)
    bin_of = jnp.sum((bin_ends[None, :] <= global_cells[:, None]).astype(jnp.int32), axis=1)
    onehot = bin_of[:, None] == jnp.arange(inner_count, dtype=jnp.int32)[None, :]
    cell_level = jnp.sum(jnp.where(onehot, wave_level[0][None, :], 0.0), axis=1) * is_live

    def loop_body(step, current):
        return one_pass(current, cell_level, energy_rate, pitch_rate)

    diffused = lax.fori_loop(0, PASSES, loop_body, cellwise)
    returned = lax.all_to_all(diffused, "inner", split_axis=0, concat_axis=2, tiled=True)
    every_cell = jnp.arange(cell_count, dtype=jnp.int32)
    owner_index = jnp.sum((owner_ends[None, :] <= every_cell[:, None]).astype(jnp.int32), axis=1)
    offset = every_cell - owner_starts[owner_index]
    position = owner_index * per_device + offset
    restored = jnp.take(returned, position, axis=2)
    return drift_step(restored, source_sector, source_tile, matrix_id, cubic_weights)


def solution(mesh):
    return jax.shard_map(
        shards,
        mesh=mesh,
        in_specs=(
            P("inner", None, "sector"),
            P("inner", None, None),
            P("inner", None, None),
            P("inner", None, None),
            P(),
            P("sector", None),
            P("sector", None),
            P(),
            P(),
        ),
        out_specs=P("inner", None, "sector"),
        check_vma=False,
    )
```

profile of v0, /device:TPU:1, one launch (start us, length us, event | category | flops | bytes accessed | tf_op | source)
XLA Modules:
  0.0 494.0 jit_solution(5908928833812959469)
XLA Ops:
  13.2 7.6 %all-to-all-start = ((f32[4,64,24,128]{3,1,0,2:T(8,128)}), f32[4,64,24,128]{3,1,0,2:T(8,128)}, u32[]{:S(2)}, u32[]{:S(2)}) async-start(f32[4,64,24,128]{3,1,0,2:T(8,128)} %bitcast_multiply_fusion.2), calls=%async_computation | async-start | bytes 6291456 | tf_op jit(solution)/shard_map/all_to_all | solution.py:35
  23.2 35.2 %all-to-all-done = f32[4,64,24,128]{3,1,0,2:T(8,128)} async-done(((f32[4,64,24,128]{3,1,0,2:T(8,128)}), f32[4,64,24,128]{3,1,0,2:T(8,128)}, u32[]{:S(2)}, u32[]{:S(2)}) %all-to-all-start) | async-done | bytes 3145760 | tf_op jit(solution)/shard_map/all_to_all | solution.py:35
  70.5 17.5 %gather_fusion.3 = f32[2048,4,64]{2,1,0:T(4,128)} fusion(f32[4,64,2048]{1,0,2:T(4,128)} %bitcast.121, s32[2048]{0:T(1024)S(1)} %fusion.11), kind=kCustom, calls=%fused_computation.3.clone | custom fusion | bytes 4202496 | tf_op jit(solution)/shard_map/jit(_take)/gather | solution.py:78
  88.0 11.7 %fusion.21 = f32[2048,4,64]{2,1,0:T(4,128)} fusion(f32[2048]{0:T(1024)S(1)} %convert_element_type.47, f32[2048,4,64]{2,1,0:T(4,128)} %gather_fusion.3, pred[2048]{0:T(1024)(128)(4,1)S(1)} %compare_and_fusion.1), kind=kLoop, calls=%fused_computation.105 | loop fusion | flops 1048576 | bytes 4204544
  99.7 6.3 %reshape.380 = f32[32,1,16384]{2,1,0:T(1,128)} reshape(f32[2048,4,64]{2,1,0:T(4,128)} %fusion.21) | data formatting | bytes 4194304
  106.0 9.8 %all-to-all-start.1 = ((f32[32,1,16384]{2,1,0:T(1,128)}), f32[32,1,16384]{2,1,0:T(1,128)S(1)}, u32[]{:S(2)}, u32[]{:S(2)}) async-start(f32[32,1,16384]{2,1,0:T(1,128)} %reshape.380), calls=%async_computation.1 | async-start | bytes 4194304 | tf_op jit(solution)/shard_map/all_to_all | solution.py:79
  117.9 46.4 %all-to-all-done.1 = f32[32,1,16384]{2,1,0:T(1,128)S(1)} async-done(((f32[32,1,16384]{2,1,0:T(1,128)}), f32[32,1,16384]{2,1,0:T(1,128)S(1)}, u32[]{:S(2)}, u32[]{:S(2)}) %all-to-all-start.1) | async-done | bytes 2097184 | tf_op jit(solution)/shard_map/all_to_all | solution.py:79
  166.1 7.3 %reduce.51 = f32[32,16384]{1,0:T(8,128)S(1)} reduce(f32[32,1,16384]{2,1,0:T(1,128)} %copy-done.4, f32[]{:T(128)} %broadcast.519), dimensions={1}, to_apply=%all_to_all.33.reduce_sub_computation | reduce | bytes 4194308 | tf_op jit(solution)/shard_map/all_to_all | solution.py:79
  182.9 146.8 %while.12 = (s32[]{:T(128)}, f32[128,64,64]{2,1,0:T(8,128)}, f32[64]{0:T(128)S(1)}, f32[128,64]{1,0:T(8,128)S(1)}, f32[128,64]{1,0:T(8,128)S(1)}, /*index=5*/s32[]{:T(128)}) while((s32[]{:T(128)}, f32[128,64,64]{2,1,0:T(8,128)}, f32[64]{0:T(128)S(1)}, f32[128,64]{1,0:T(8,128)S(1)}, f32[128,64]{1,0:T(8,128)S(1)}, /*index=5*/s32[]{:T(128)}) %tuple.96), condition=%wide.region_7.12_spmd, body=%wide.region_6.11_spmd.sunk | while | flops 4694018 | bytes 37617276 | solution.py:90
  182.9 5.5 %subtract_multiply_fusion.4 = f32[128,63,64]{2,1,0:T(8,128)S(1)} fusion(f32[128,64,64]{2,1,0:T(8,128)} %get-tuple-element.209, f32[128,63]{1,0:T(8,128)S(1)} %bitcast.128), kind=kLoop, calls=%fused_computation.8.clone.1 | loop fusion | flops 1032192 | bytes 6225408 | tf_op jit(solution)/shard_map/while/body/eval_jaxpr/mul | solution.py:48
  195.1 5.5 %subtract_multiply_fusion.4 = f32[128,63,64]{2,1,0:T(8,128)S(1)} fusion(f32[128,64,64]{2,1,0:T(8,128)} %get-tuple-element.209, f32[128,63]{1,0:T(8,128)S(1)} %bitcast.128), kind=kLoop, calls=%fused_computation.8.clone.1 | loop fusion | flops 1032192 | bytes 6225408 | tf_op jit(solution)/shard_map/while/body/eval_jaxpr/mul | solution.py:48
  207.4 5.5 %subtract_multiply_fusion.4 = f32[128,63,64]{2,1,0:T(8,128)S(1)} fusion(f32[128,64,64]{2,1,0:T(8,128)} %get-tuple-element.209, f32[128,63]{1,0:T(8,128)S(1)} %bitcast.128), kind=kLoop, calls=%fused_computation.8.clone.1 | loop fusion | flops 1032192 | bytes 6225408 | tf_op jit(solution)/shard_map/while/body/eval_jaxpr/mul | solution.py:48
  219.6 5.5 %subtract_multiply_fusion.4 = f32[128,63,64]{2,1,0:T(8,128)S(1)} fusion(f32[128,64,64]{2,1,0:T(8,128)} %get-tuple-element.209, f32[128,63]{1,0:T(8,128)S(1)} %bitcast.128), kind=kLoop, calls=%fused_computation.8.clone.1 | loop fusion | flops 1032192 | bytes 6225408 | tf_op jit(solution)/shard_map/while/body/eval_jaxpr/mul | solution.py:48
  231.8 5.5 %subtract_multiply_fusion.4 = f32[128,63,64]{2,1,0:T(8,128)S(1)} fusion(f32[128,64,64]{2,1,0:T(8,128)} %get-tuple-element.209, f32[128,63]{1,0:T(8,128)S(1)} %bitcast.128), kind=kLoop, calls=%fused_computation.8.clone.1 | loop fusion | flops 1032192 | bytes 6225408 | tf_op jit(solution)/shard_map/while/body/eval_jaxpr/mul | solution.py:48
  244.1 5.5 %subtract_multiply_fusion.4 = f32[128,63,64]{2,1,0:T(8,128)S(1)} fusion(f32[128,64,64]{2,1,0:T(8,128)} %get-tuple-element.209, f32[128,63]{1,0:T(8,128)S(1)} %bitcast.128), kind=kLoop, calls=%fused_computation.8.clone.1 | loop fusion | flops 1032192 | bytes 6225408 | tf_op jit(solution)/shard_map/while/body/eval_jaxpr/mul | solution.py:48
  256.3 5.5 %subtract_multiply_fusion.4 = f32[128,63,64]{2,1,0:T(8,128)S(1)} fusion(f32[128,64,64]{2,1,0:T(8,128)} %get-tuple-element.209, f32[128,63]{1,0:T(8,128)S(1)} %bitcast.128), kind=kLoop, calls=%fused_computation.8.clone.1 | loop fusion | flops 1032192 | bytes 6225408 | tf_op jit(solution)/shard_map/while/body/eval_jaxpr/mul | solution.py:48
  268.5 5.5 %subtract_multiply_fusion.4 = f32[128,63,64]{2,1,0:T(8,128)S(1)} fusion(f32[128,64,64]{2,1,0:T(8,128)} %get-tuple-element.209, f32[128,63]{1,0:T(8,128)S(1)} %bitcast.128), kind=kLoop, calls=%fused_computation.8.clone.1 | loop fusion | flops 1032192 | bytes 6225408 | tf_op jit(solution)/shard_map/while/body/eval_jaxpr/mul | solution.py:48
  335.2 7.5 %all-to-all-start.2 = ((f32[32,1,16384]{2,1,0:T(1,128)}), f32[32,1,16384]{2,1,0:T(1,128)}, u32[]{:S(2)}, u32[]{:S(2)}) async-start(f32[32,1,16384]{2,1,0:T(1,128)} %reshape.382), calls=%async_computation.2 | async-start | bytes 4194304 | tf_op jit(solution)/shard_map/all_to_all | solution.py:91
  348.6 15.5 %compare_and_fusion = (pred[2048]{0:T(1024)(128)(4,1)S(1)}, s32[2048]{0:T(1024)S(1)}) fusion(pred[2048]{0:T(1024)(128)(4,1)S(1)} %get-tuple-element.119, pred[2048]{0:T(1024)(128)(4,1)S(1)} %get-tuple-element.118, pred[2048]{0:T(1024)(128)(4,1)S(1)} %get-tuple-element.117, pred[2048]{0:T(1024)(128)(4,1)S(1)} %get-tuple-element.116, ...), kind=kLoop, calls=%fused_computation.74 | loop fusion | flops 69632 | bytes 77924 | tf_op jit(solution)/shard_map/jit(_take)/and | solution.py:96
  364.1 27.0 %all-to-all-done.2 = f32[32,1,16384]{2,1,0:T(1,128)} async-done(((f32[32,1,16384]{2,1,0:T(1,128)}), f32[32,1,16384]{2,1,0:T(1,128)}, u32[]{:S(2)}, u32[]{:S(2)}) %all-to-all-start.2) | async-done | bytes 2097184 | tf_op jit(solution)/shard_map/all_to_all | solution.py:91
  391.1 7.3 %reduce.52 = f32[32,16384]{1,0:T(8,128)S(1)} reduce(f32[32,1,16384]{2,1,0:T(1,128)} %all-to-all-done.2, f32[]{:T(128)} %broadcast.519), dimensions={1}, to_apply=%all_to_all.37.reduce_sub_computation | reduce | bytes 4194308 | tf_op jit(solution)/shard_map/all_to_all | solution.py:91
  406.7 17.5 %gather_fusion.4 = f32[2048,4,64]{2,1,0:T(4,128)} fusion(f32[4,64,2048]{1,0,2:T(4,128)} %bitcast.122, s32[2048]{0:T(1024)S(1)} %broadcast_clamp_fusion), kind=kCustom, calls=%fused_computation.6.clone | custom fusion | bytes 4202496 | tf_op jit(solution)/shard_map/jit(_take)/gather | solution.py:96
  424.2 10.9 %broadcast_select_fusion = f32[2048,4,64]{2,1,0:T(4,128)} fusion(f32[2048,4,64]{2,1,0:T(4,128)} %gather_fusion.4, pred[2048]{0:T(1024)(128)(4,1)S(1)} %get-tuple-element.130), kind=kLoop, calls=%fused_computation.15 | loop fusion | flops 524288 | bytes 4196352 | tf_op jit(solution)/shard_map/jit(_take)/select_n | solution.py:96
  443.4 42.2 %all_to_all.46 = f32[4,64,24,128]{3,1,0,2:T(8,128)S(1)} all-to-all(f32[4,64,24,128]{3,1,0,2:T(8,128)S(1)} %bitcast_multiply_fusion.1), channel_id=1, replica_groups=mesh['sector'=8,'inner'=32] {'sector'}, dimensions={2} | all-to-all | bytes 6291456 | tf_op jit(solution)/shard_map/all_to_all | solution.py:35
  (156 shorter events, 179.6 us)
Async XLA Ops:
  0.0 3.1 copy-start
  13.2 8.6 %copy-start.5 = (f32[32,128,128]{2,1,0:T(8,128)S(1)}, f32[32,128,128]{2,1,0:T(8,128)}, u32[]{:S(2)}) copy-start(f32[32,128,128]{2,1,0:T(8,128)} %param.23) | copy-start | bytes 6291460
  13.2 45.2 %all-to-all-start = ((f32[4,64,24,128]{3,1,0,2:T(8,128)}), f32[4,64,24,128]{3,1,0,2:T(8,128)}, u32[]{:S(2)}, u32[]{:S(2)}) async-start(f32[4,64,24,128]{3,1,0,2:T(8,128)} %bitcast_multiply_fusion.2), calls=%async_computation | async-start | bytes 6291456 | tf_op jit(solution)/shard_map/all_to_all | solution.py:35
  106.0 9.8 %copy-start.8 = (s32[1,32]{1,0:T(1,128)S(1)}, s32[1,32]{1,0:T(1,128)}, u32[]{:S(2)}) copy-start(s32[1,32]{1,0:T(1,128)} %param.24) | copy-start | bytes 388
  106.0 10.1 %copy-start.6 = (f32[128,64]{0,1:T(8,128)S(1)}, f32[128,64]{0,1:T(8,128)}, u32[]{:S(2)}) copy-start(f32[128,64]{0,1:T(8,128)} %param.26) | copy-start | bytes 98308
  106.0 10.2 %copy-start.7 = (f32[128,64]{0,1:T(8,128)S(1)}, f32[128,64]{0,1:T(8,128)}, u32[]{:S(2)}) copy-start(f32[128,64]{0,1:T(8,128)} %param.27) | copy-start | bytes 98308
  106.0 11.8 %copy-start.9 = (f32[1,32]{1,0:T(1,128)S(1)}, f32[1,32]{1,0:T(1,128)}, u32[]{:S(2)}) copy-start(f32[1,32]{1,0:T(1,128)} %param.25) | copy-start | bytes 388
  106.0 58.3 %all-to-all-start.1 = ((f32[32,1,16384]{2,1,0:T(1,128)}), f32[32,1,16384]{2,1,0:T(1,128)S(1)}, u32[]{:S(2)}, u32[]{:S(2)}) async-start(f32[32,1,16384]{2,1,0:T(1,128)} %reshape.380), calls=%async_computation.1 | async-start | bytes 4194304 | tf_op jit(solution)/shard_map/all_to_all | solution.py:79
  182.9 5.5 %copy-start.2 = (f32[128,64,64]{2,1,0:T(8,128)S(1)}, f32[128,64,64]{2,1,0:T(8,128)}, u32[]{:S(2)}) copy-start(f32[128,64,64]{2,1,0:T(8,128)} %get-tuple-element.209) | copy-start | bytes 6291460 | tf_op jit(solution)/shard_map/while
  193.2 1.9 copy-start.3
  195.1 5.5 %copy-start.2 = (f32[128,64,64]{2,1,0:T(8,128)S(1)}, f32[128,64,64]{2,1,0:T(8,128)}, u32[]{:S(2)}) copy-start(f32[128,64,64]{2,1,0:T(8,128)} %get-tuple-element.209) | copy-start | bytes 6291460 | tf_op jit(solution)/shard_map/while
  207.4 5.5 %copy-start.2 = (f32[128,64,64]{2,1,0:T(8,128)S(1)}, f32[128,64,64]{2,1,0:T(8,128)}, u32[]{:S(2)}) copy-start(f32[128,64,64]{2,1,0:T(8,128)} %get-tuple-element.209) | copy-start | bytes 6291460 | tf_op jit(solution)/shard_map/while
  217.7 1.9 copy-start.3
  219.6 5.5 %copy-start.2 = (f32[128,64,64]{2,1,0:T(8,128)S(1)}, f32[128,64,64]{2,1,0:T(8,128)}, u32[]{:S(2)}) copy-start(f32[128,64,64]{2,1,0:T(8,128)} %get-tuple-element.209) | copy-start | bytes 6291460 | tf_op jit(solution)/shard_map/while
  231.8 5.5 %copy-start.2 = (f32[128,64,64]{2,1,0:T(8,128)S(1)}, f32[128,64,64]{2,1,0:T(8,128)}, u32[]{:S(2)}) copy-start(f32[128,64,64]{2,1,0:T(8,128)} %get-tuple-element.209) | copy-start | bytes 6291460 | tf_op jit(solution)/shard_map/while
  244.1 5.5 %copy-start.2 = (f32[128,64,64]{2,1,0:T(8,128)S(1)}, f32[128,64,64]{2,1,0:T(8,128)}, u32[]{:S(2)}) copy-start(f32[128,64,64]{2,1,0:T(8,128)} %get-tuple-element.209) | copy-start | bytes 6291460 | tf_op jit(solution)/shard_map/while
  256.3 5.5 %copy-start.2 = (f32[128,64,64]{2,1,0:T(8,128)S(1)}, f32[128,64,64]{2,1,0:T(8,128)}, u32[]{:S(2)}) copy-start(f32[128,64,64]{2,1,0:T(8,128)} %get-tuple-element.209) | copy-start | bytes 6291460 | tf_op jit(solution)/shard_map/while
  268.5 5.5 %copy-start.2 = (f32[128,64,64]{2,1,0:T(8,128)S(1)}, f32[128,64,64]{2,1,0:T(8,128)}, u32[]{:S(2)}) copy-start(f32[128,64,64]{2,1,0:T(8,128)} %get-tuple-element.209) | copy-start | bytes 6291460 | tf_op jit(solution)/shard_map/while
  280.8 5.5 %copy-start.2 = (f32[128,64,64]{2,1,0:T(8,128)S(1)}, f32[128,64,64]{2,1,0:T(8,128)}, u32[]{:S(2)}) copy-start(f32[128,64,64]{2,1,0:T(8,128)} %get-tuple-element.209) | copy-start | bytes 6291460 | tf_op jit(solution)/shard_map/while
  293.0 5.5 %copy-start.2 = (f32[128,64,64]{2,1,0:T(8,128)S(1)}, f32[128,64,64]{2,1,0:T(8,128)}, u32[]{:S(2)}) copy-start(f32[128,64,64]{2,1,0:T(8,128)} %get-tuple-element.209) | copy-start | bytes 6291460 | tf_op jit(solution)/shard_map/while
  305.3 5.5 %copy-start.2 = (f32[128,64,64]{2,1,0:T(8,128)S(1)}, f32[128,64,64]{2,1,0:T(8,128)}, u32[]{:S(2)}) copy-start(f32[128,64,64]{2,1,0:T(8,128)} %get-tuple-element.209) | copy-start | bytes 6291460 | tf_op jit(solution)/shard_map/while
  317.5 5.5 %copy-start.2 = (f32[128,64,64]{2,1,0:T(8,128)S(1)}, f32[128,64,64]{2,1,0:T(8,128)}, u32[]{:S(2)}) copy-start(f32[128,64,64]{2,1,0:T(8,128)} %get-tuple-element.209) | copy-start | bytes 6291460 | tf_op jit(solution)/shard_map/while
  335.2 55.9 %all-to-all-start.2 = ((f32[32,1,16384]{2,1,0:T(1,128)}), f32[32,1,16384]{2,1,0:T(1,128)}, u32[]{:S(2)}, u32[]{:S(2)}) async-start(f32[32,1,16384]{2,1,0:T(1,128)} %reshape.382), calls=%async_computation.2 | async-start | bytes 4194304 | tf_op jit(solution)/shard_map/all_to_all | solution.py:91
  490.3 3.7 copy-start.1
  (11 other events, 20.6 us)
where the time goes:
time: 496 us; the launch traced here: 494 us
  other arithmetic  194 us (39%)
  local copies, waits for them, and re-layouts  120 us (24%)
  waiting for transfers between devices  109 us (22%)
  blocking collectives  42.2 us (9%)
  starting transfers between devices  24.9 us (5%)
    mul x12, other arithmetic, one_pass(): flux_p = pitch_rate[:, :-1, None] * (field[:, 1:] - field[:, :-1])  65.8 us
    all_to_all x1, waiting for transfers between devices, shards(): lax.all_to_all(packed, 'inner', split_axis=2, concat_axis=0, tiled=True)  46.4 us
    all_to_all x1, blocking collectives, drift_step(): lax.all_to_all(outgoing, 'sector', split_axis=2, concat_axis=2, tiled=True)  42.2 us
    add x12, other arithmetic, one_pass(): return field + rate_cell[None, None, :] * (change_e + change_p)  35.7 us
    all_to_all x1, waiting for transfers between devices, drift_step(): lax.all_to_all(outgoing, 'sector', split_axis=2, concat_axis=2, tiled=True)  35.2 us
    all_to_all x1, waiting for transfers between devices, shards(): lax.all_to_all(diffused, 'inner', split_axis=0, concat_axis=2, tiled=True)  27 us
    while x48, local copies, waits for them, and re-layouts  23.1 us
    mul x12, other arithmetic, one_pass(): flux_e = energy_rate[:-1, :, None] * (field[1:] - field[:-1])  21.8 us
  transfers between devices with their start and end apart: 3, of which 3 were waited for; matrix products, arithmetic and copies ran while one was open for 5% of the time, Pallas kernels for 0%

commit v1 on v0

--- a/solution.py
+++ b/solution.py
@@ -76,7 +76,10 @@
     valid = (offsets[None, :] < owner_cells[:, None]).reshape(-1).astype(jnp.float32)
     clipped = jnp.minimum(cell_index, cell_count - 1).reshape(-1)
     packed = jnp.take(first, clipped, axis=2) * valid[None, None, :]
-    cellwise = lax.all_to_all(packed, "inner", split_axis=2, concat_axis=0, tiled=True)
+    cellwise = jnp.concatenate(
+        lax.all_to_all(jnp.stack(jnp.split(packed, lax.axis_size("inner"), axis=2)), "inner", 0, 0),
+        axis=0,
+    )
     bin_ends = jnp.cumsum(lengths)
     global_cells = owner_starts[inner_here] + offsets
     is_live = (offsets < owner_cells[inner_here]).astype(jnp.float32)

time: 496 us -> 494 us (level)
  blocking collectives: 42.2 us -> 99.1 us
  waiting for transfers between devices: 109 us -> 59.3 us
  starting transfers between devices: 24.9 us -> 17.1 us
  other arithmetic: 194 us -> 188 us
    all_to_all x0 -> x1, blocking collectives: none -> 54.6 us  [shards(): lax.all_to_all(diffused, 'inner', split_axis=0, concat_axis=2, tiled=True)]
    mul x12, other arithmetic: 65.8 us -> 17 us  [one_pass(): flux_p = pitch_rate[:, :-1, None] * (field[:, 1:] - field[:, :-1])]
    mul x12, other arithmetic: 21.8 us -> 65.6 us  [one_pass(): flux_e = energy_rate[:-1, :, None] * (field[1:] - field[:-1])]
    all_to_all x2 -> x1, waiting for transfers between devices: 73.4 us -> 47.2 us  [shards(): lax.all_to_all(jnp.stack(jnp.split(packed, lax.axis_size('inner'), axis=2...]
    all_to_all x1, waiting for transfers between devices: 35.2 us -> 12.1 us  [drift_step(): lax.all_to_all(outgoing, 'sector', split_axis=2, concat_axis=2, tiled=True)]
    unnamed x1 -> x0, other arithmetic: 11.7 us -> none
    mul x0 -> x1, other arithmetic: none -> 10.9 us  [shards(): packed = jnp.take(first, clipped, axis=2) * valid[None, None, :]]
    all_to_all x2 -> x1, starting transfers between devices: 17.2 us -> 9.63 us  [shards(): lax.all_to_all(jnp.stack(jnp.split(packed, lax.axis_size('inner'), axis=2...]
  transfers between devices with their start and end apart: 3 -> 2, of which waited for: 3 -> 2; matrix products, arithmetic and copies ran while one was open for 5% -> 5% of each run, Pallas kernels for 0% -> 0%
where the time goes in v1:
time: 494 us; the launch traced here: 492 us
  other arithmetic  188 us (38%)
  local copies, waits for them, and re-layouts  123 us (25%)
  blocking collectives  99.1 us (20%)
  waiting for transfers between devices  59.3 us (12%)
  starting transfers between devices  17.1 us (3%)
    mul x12, other arithmetic, one_pass(): flux_e = energy_rate[:-1, :, None] * (field[1:] - field[:-1])  65.6 us
    all_to_all x1, blocking collectives, shards(): lax.all_to_all(diffused, 'inner', split_axis=0, concat_axis=2, tiled=True)  54.6 us
    all_to_all x1, waiting for transfers between devices, shards(): lax.all_to_all(jnp.stack(jnp.split(packed, lax.axis_size('inner'), axis=2...  47.2 us
    all_to_all x1, blocking collectives, drift_step(): lax.all_to_all(outgoing, 'sector', split_axis=2, concat_axis=2, tiled=True)  44.5 us
    add x12, other arithmetic, one_pass(): return field + rate_cell[None, None, :] * (change_e + change_p)  35.7 us
    while x48, local copies, waits for them, and re-layouts  23.1 us
    unnamed x51, local copies, waits for them, and re-layouts  22 us
    gather x1, local copies, waits for them, and re-layouts, shards(): packed = jnp.take(first, clipped, axis=2) * valid[None, None, :]  17.5 us
  transfers between devices with their start and end apart: 2, of which 2 were waited for; matrix products, arithmetic and copies ran while one was open for 5% of the time, Pallas kernels for 0%

profile of v1, /device:TPU:1, one launch (start us, length us, event | category | flops | bytes accessed | tf_op | source)
XLA Modules:
  0.0 491.8 jit_solution(6471826953418503344)
XLA Ops:
  13.9 7.5 %all-to-all-start = ((f32[4,64,24,128]{3,1,0,2:T(8,128)}), f32[4,64,24,128]{3,1,0,2:T(8,128)}, u32[]{:S(2)}, u32[]{:S(2)}) async-start(f32[4,64,24,128]{3,1,0,2:T(8,128)} %bitcast_multiply_fusion.2), calls=%async_computation | async-start | bytes 6291456 | tf_op jit(solution)/shard_map/all_to_all | solution.py:35
  31.2 15.7 %compare_and_fusion = (pred[2048]{0:T(1024)(128)(4,1)S(1)}, s32[2048]{0:T(1024)S(1)}) fusion(pred[2048]{0:T(1024)(128)(4,1)S(1)} %get-tuple-element.119, pred[2048]{0:T(1024)(128)(4,1)S(1)} %get-tuple-element.118, pred[2048]{0:T(1024)(128)(4,1)S(1)} %get-tuple-element.117, pred[2048]{0:T(1024)(128)(4,1)S(1)} %get-tuple-element.116, ...), kind=kLoop, calls=%fused_computation.138 | loop fusion | flops 69632 | bytes 77924 | tf_op jit(solution)/shard_map/jit(_take)/and | solution.py:99
  46.9 12.1 %all-to-all-done = f32[4,64,24,128]{3,1,0,2:T(8,128)} async-done(((f32[4,64,24,128]{3,1,0,2:T(8,128)}), f32[4,64,24,128]{3,1,0,2:T(8,128)}, u32[]{:S(2)}, u32[]{:S(2)}) %all-to-all-start) | async-done | bytes 3145760 | tf_op jit(solution)/shard_map/all_to_all | solution.py:35
  71.1 17.5 %gather_fusion.3 = f32[2048,4,64]{2,1,0:T(4,128)} fusion(f32[4,64,2048]{1,0,2:T(4,128)} %bitcast.242, s32[2048]{0:T(1024)S(1)} %get-tuple-element.171), kind=kCustom, calls=%fused_computation.3.clone | custom fusion | bytes 4202496 | tf_op jit(solution)/shard_map/jit(_take)/gather | solution.py:78
  88.6 10.9 %bitcast_multiply_fusion = f32[4,64,2048]{1,0,2:T(4,128)S(1)} fusion(f32[2048,4,64]{2,1,0:T(4,128)} %gather_fusion.3, f32[2048]{0:T(1024)S(1)} %convert_element_type.47, pred[2048]{0:T(1024)(128)(4,1)S(1)} %compare_and_fusion.1), kind=kLoop, calls=%fused_computation.10 | loop fusion | flops 1048576 | bytes 4204544 | tf_op jit(solution)/shard_map/mul | solution.py:78
  102.3 6.3 %reshape.384 = f32[32,1,16384]{2,1,0:T(1,128)} reshape(f32[32,64,4,64]{3,2,1,0:T(4,128)} %bitcast.248) | data formatting | bytes 4194304
  108.6 9.6 %all-to-all-start.1 = ((f32[32,1,16384]{2,1,0:T(1,128)}), f32[32,1,16384]{2,1,0:T(1,128)S(1)}, u32[]{:S(2)}, u32[]{:S(2)}) async-start(f32[32,1,16384]{2,1,0:T(1,128)} %reshape.384), calls=%async_computation.1 | async-start | bytes 4194304 | tf_op jit(solution)/shard_map/all_to_all | solution.py:80
  119.6 47.2 %all-to-all-done.1 = f32[32,1,16384]{2,1,0:T(1,128)S(1)} async-done(((f32[32,1,16384]{2,1,0:T(1,128)}), f32[32,1,16384]{2,1,0:T(1,128)S(1)}, u32[]{:S(2)}, u32[]{:S(2)}) %all-to-all-start.1) | async-done | bytes 2097184 | tf_op jit(solution)/shard_map/all_to_all | solution.py:80
  168.6 7.4 %reduce.51 = f32[32,16384]{1,0:T(8,128)S(1)} reduce(f32[32,1,16384]{2,1,0:T(1,128)} %copy-done.4, f32[]{:T(128)} %broadcast.515), dimensions={1}, to_apply=%all_to_all.23.reduce_sub_computation | reduce | bytes 4194308 | tf_op jit(solution)/shard_map/all_to_all | solution.py:80
  185.5 142.0 %while.12 = (s32[]{:T(128)}, f32[128,64,64]{2,1,0:T(8,128)}, f32[64]{0:T(128)S(1)}, f32[128,64]{1,0:T(8,128)S(1)}, f32[128,64]{1,0:T(8,128)S(1)}, /*index=5*/s32[]{:T(128)}) while((s32[]{:T(128)}, f32[128,64,64]{2,1,0:T(8,128)}, f32[64]{0:T(128)S(1)}, f32[128,64]{1,0:T(8,128)S(1)}, f32[128,64]{1,0:T(8,128)S(1)}, /*index=5*/s32[]{:T(128)}) %tuple.98), condition=%wide.region_7.12_spmd, body=%wide.region_6.11_spmd.sunk | while | flops 4694018 | bytes 37617276 | solution.py:93
  185.5 5.5 %subtract_multiply_fusion.5 = f32[127,64,64]{2,1,0:T(8,128)S(1)} fusion(f32[128,64,64]{2,1,0:T(8,128)} %get-tuple-element.213, f32[127,64]{1,0:T(8,128)S(1)} %bitcast.249), kind=kLoop, calls=%fused_computation.9.clone.1 | loop fusion | flops 1040384 | bytes 6274816 | tf_op jit(solution)/shard_map/while/body/eval_jaxpr/mul | solution.py:47
  197.3 5.5 %subtract_multiply_fusion.5 = f32[127,64,64]{2,1,0:T(8,128)S(1)} fusion(f32[128,64,64]{2,1,0:T(8,128)} %get-tuple-element.213, f32[127,64]{1,0:T(8,128)S(1)} %bitcast.249), kind=kLoop, calls=%fused_computation.9.clone.1 | loop fusion | flops 1040384 | bytes 6274816 | tf_op jit(solution)/shard_map/while/body/eval_jaxpr/mul | solution.py:47
  209.1 5.5 %subtract_multiply_fusion.5 = f32[127,64,64]{2,1,0:T(8,128)S(1)} fusion(f32[128,64,64]{2,1,0:T(8,128)} %get-tuple-element.213, f32[127,64]{1,0:T(8,128)S(1)} %bitcast.249), kind=kLoop, calls=%fused_computation.9.clone.1 | loop fusion | flops 1040384 | bytes 6274816 | tf_op jit(solution)/shard_map/while/body/eval_jaxpr/mul | solution.py:47
  221.0 5.5 %subtract_multiply_fusion.5 = f32[127,64,64]{2,1,0:T(8,128)S(1)} fusion(f32[128,64,64]{2,1,0:T(8,128)} %get-tuple-element.213, f32[127,64]{1,0:T(8,128)S(1)} %bitcast.249), kind=kLoop, calls=%fused_computation.9.clone.1 | loop fusion | flops 1040384 | bytes 6274816 | tf_op jit(solution)/shard_map/while/body/eval_jaxpr/mul | solution.py:47
  232.8 5.5 %subtract_multiply_fusion.5 = f32[127,64,64]{2,1,0:T(8,128)S(1)} fusion(f32[128,64,64]{2,1,0:T(8,128)} %get-tuple-element.213, f32[127,64]{1,0:T(8,128)S(1)} %bitcast.249), kind=kLoop, calls=%fused_computation.9.clone.1 | loop fusion | flops 1040384 | bytes 6274816 | tf_op jit(solution)/shard_map/while/body/eval_jaxpr/mul | solution.py:47
  244.6 5.5 %subtract_multiply_fusion.5 = f32[127,64,64]{2,1,0:T(8,128)S(1)} fusion(f32[128,64,64]{2,1,0:T(8,128)} %get-tuple-element.213, f32[127,64]{1,0:T(8,128)S(1)} %bitcast.249), kind=kLoop, calls=%fused_computation.9.clone.1 | loop fusion | flops 1040384 | bytes 6274816 | tf_op jit(solution)/shard_map/while/body/eval_jaxpr/mul | solution.py:47
  256.4 5.5 %subtract_multiply_fusion.5 = f32[127,64,64]{2,1,0:T(8,128)S(1)} fusion(f32[128,64,64]{2,1,0:T(8,128)} %get-tuple-element.213, f32[127,64]{1,0:T(8,128)S(1)} %bitcast.249), kind=kLoop, calls=%fused_computation.9.clone.1 | loop fusion | flops 1040384 | bytes 6274816 | tf_op jit(solution)/shard_map/while/body/eval_jaxpr/mul | solution.py:47
  268.3 5.5 %subtract_multiply_fusion.5 = f32[127,64,64]{2,1,0:T(8,128)S(1)} fusion(f32[128,64,64]{2,1,0:T(8,128)} %get-tuple-element.213, f32[127,64]{1,0:T(8,128)S(1)} %bitcast.249), kind=kLoop, calls=%fused_computation.9.clone.1 | loop fusion | flops 1040384 | bytes 6274816 | tf_op jit(solution)/shard_map/while/body/eval_jaxpr/mul | solution.py:47
  315.6 5.5 %subtract_multiply_fusion.5 = f32[127,64,64]{2,1,0:T(8,128)S(1)} fusion(f32[128,64,64]{2,1,0:T(8,128)} %get-tuple-element.213, f32[127,64]{1,0:T(8,128)S(1)} %bitcast.249), kind=kLoop, calls=%fused_computation.9.clone.1 | loop fusion | flops 1040384 | bytes 6274816 | tf_op jit(solution)/shard_map/while/body/eval_jaxpr/mul | solution.py:47
  331.9 54.6 %all_to_all.33 = f32[32,1,16384]{2,1,0:T(1,128)} all-to-all(f32[32,1,16384]{2,1,0:T(1,128)S(1)} %reshape.386), channel_id=1, replica_groups=mesh['sector'=8,'inner'=32] {'inner'}, dimensions={0} | all-to-all | bytes 4194304 | tf_op jit(solution)/shard_map/all_to_all | solution.py:94
  386.6 7.4 %reduce.52 = f32[32,16384]{1,0:T(8,128)S(1)} reduce(f32[32,1,16384]{2,1,0:T(1,128)} %all_to_all.33, f32[]{:T(128)} %broadcast.515), dimensions={1}, to_apply=%all_to_all.24.reduce_sub_computation | reduce | bytes 4194308 | tf_op jit(solution)/shard_map/all_to_all | solution.py:94
  402.3 17.5 %gather_fusion.4 = f32[2048,4,64]{2,1,0:T(4,128)} fusion(f32[4,64,2048]{1,0,2:T(4,128)} %bitcast.243, s32[2048]{0:T(1024)S(1)} %get-tuple-element.172), kind=kCustom, calls=%fused_computation.6.clone | custom fusion | bytes 4202496 | tf_op jit(solution)/shard_map/jit(_take)/gather | solution.py:99
  419.8 10.9 %broadcast_select_fusion = f32[2048,4,64]{2,1,0:T(4,128)} fusion(f32[2048,4,64]{2,1,0:T(4,128)} %gather_fusion.4, pred[2048]{0:T(1024)(128)(4,1)S(1)} %get-tuple-element.130), kind=kLoop, calls=%fused_computation.15 | loop fusion | flops 524288 | bytes 4196352 | tf_op jit(solution)/shard_map/jit(_take)/select_n | solution.py:99
  439.0 44.5 %all_to_all.34 = f32[4,64,24,128]{3,1,0,2:T(8,128)S(1)} all-to-all(f32[4,64,24,128]{3,1,0,2:T(8,128)S(1)} %bitcast_multiply_fusion.1), channel_id=1, replica_groups=mesh['sector'=8,'inner'=32] {'sector'}, dimensions={2} | all-to-all | bytes 6291456 | tf_op jit(solution)/shard_map/all_to_all | solution.py:35
  (185 shorter events, 172.4 us)
Async XLA Ops:
  0.0 3.3 copy-start
  13.9 45.1 %all-to-all-start = ((f32[4,64,24,128]{3,1,0,2:T(8,128)}), f32[4,64,24,128]{3,1,0,2:T(8,128)}, u32[]{:S(2)}, u32[]{:S(2)}) async-start(f32[4,64,24,128]{3,1,0,2:T(8,128)} %bitcast_multiply_fusion.2), calls=%async_computation | async-start | bytes 6291456 | tf_op jit(solution)/shard_map/all_to_all | solution.py:35
  102.3 16.0 %copy-start.8 = (s32[1,32]{1,0:T(1,128)S(1)}, s32[1,32]{1,0:T(1,128)}, u32[]{:S(2)}) copy-start(s32[1,32]{1,0:T(1,128)} %param.24) | copy-start | bytes 388
  102.3 16.3 %copy-start.6 = (f32[128,64]{0,1:T(8,128)S(1)}, f32[128,64]{0,1:T(8,128)}, u32[]{:S(2)}) copy-start(f32[128,64]{0,1:T(8,128)} %param.26) | copy-start | bytes 98308
  102.3 16.4 %copy-start.7 = (f32[128,64]{0,1:T(8,128)S(1)}, f32[128,64]{0,1:T(8,128)}, u32[]{:S(2)}) copy-start(f32[128,64]{0,1:T(8,128)} %param.27) | copy-start | bytes 98308
  102.3 17.2 %copy-start.9 = (f32[1,32]{1,0:T(1,128)S(1)}, f32[1,32]{1,0:T(1,128)}, u32[]{:S(2)}) copy-start(f32[1,32]{1,0:T(1,128)} %param.25) | copy-start | bytes 388
  108.6 58.1 %all-to-all-start.1 = ((f32[32,1,16384]{2,1,0:T(1,128)}), f32[32,1,16384]{2,1,0:T(1,128)S(1)}, u32[]{:S(2)}, u32[]{:S(2)}) async-start(f32[32,1,16384]{2,1,0:T(1,128)} %reshape.384), calls=%async_computation.1 | async-start | bytes 4194304 | tf_op jit(solution)/shard_map/all_to_all | solution.py:80
  185.5 5.5 %copy-start.2 = (f32[128,64,64]{2,1,0:T(8,128)S(1)}, f32[128,64,64]{2,1,0:T(8,128)}, u32[]{:S(2)}) copy-start(f32[128,64,64]{2,1,0:T(8,128)} %get-tuple-element.213) | copy-start | bytes 6291460 | tf_op jit(solution)/shard_map/while
  195.4 1.9 copy-start.3
  197.3 5.5 %copy-start.2 = (f32[128,64,64]{2,1,0:T(8,128)S(1)}, f32[128,64,64]{2,1,0:T(8,128)}, u32[]{:S(2)}) copy-start(f32[128,64,64]{2,1,0:T(8,128)} %get-tuple-element.213) | copy-start | bytes 6291460 | tf_op jit(solution)/shard_map/while
  209.1 5.5 %copy-start.2 = (f32[128,64,64]{2,1,0:T(8,128)S(1)}, f32[128,64,64]{2,1,0:T(8,128)}, u32[]{:S(2)}) copy-start(f32[128,64,64]{2,1,0:T(8,128)} %get-tuple-element.213) | copy-start | bytes 6291460 | tf_op jit(solution)/shard_map/while
  221.0 5.5 %copy-start.2 = (f32[128,64,64]{2,1,0:T(8,128)S(1)}, f32[128,64,64]{2,1,0:T(8,128)}, u32[]{:S(2)}) copy-start(f32[128,64,64]{2,1,0:T(8,128)} %get-tuple-element.213) | copy-start | bytes 6291460 | tf_op jit(solution)/shard_map/while
  230.9 1.9 copy-start.3
  232.8 5.5 %copy-start.2 = (f32[128,64,64]{2,1,0:T(8,128)S(1)}, f32[128,64,64]{2,1,0:T(8,128)}, u32[]{:S(2)}) copy-start(f32[128,64,64]{2,1,0:T(8,128)} %get-tuple-element.213) | copy-start | bytes 6291460 | tf_op jit(solution)/shard_map/while
  242.7 1.9 copy-start.3
  244.6 5.5 %copy-start.2 = (f32[128,64,64]{2,1,0:T(8,128)S(1)}, f32[128,64,64]{2,1,0:T(8,128)}, u32[]{:S(2)}) copy-start(f32[128,64,64]{2,1,0:T(8,128)} %get-tuple-element.213) | copy-start | bytes 6291460 | tf_op jit(solution)/shard_map/while
  256.4 5.5 %copy-start.2 = (f32[128,64,64]{2,1,0:T(8,128)S(1)}, f32[128,64,64]{2,1,0:T(8,128)}, u32[]{:S(2)}) copy-start(f32[128,64,64]{2,1,0:T(8,128)} %get-tuple-element.213) | copy-start | bytes 6291460 | tf_op jit(solution)/shard_map/while
  266.3 1.9 copy-start.3
  268.3 5.5 %copy-start.2 = (f32[128,64,64]{2,1,0:T(8,128)S(1)}, f32[128,64,64]{2,1,0:T(8,128)}, u32[]{:S(2)}) copy-start(f32[128,64,64]{2,1,0:T(8,128)} %get-tuple-element.213) | copy-start | bytes 6291460 | tf_op jit(solution)/shard_map/while
  280.1 5.5 %copy-start.2 = (f32[128,64,64]{2,1,0:T(8,128)S(1)}, f32[128,64,64]{2,1,0:T(8,128)}, u32[]{:S(2)}) copy-start(f32[128,64,64]{2,1,0:T(8,128)} %get-tuple-element.213) | copy-start | bytes 6291460 | tf_op jit(solution)/shard_map/while
  291.9 5.5 %copy-start.2 = (f32[128,64,64]{2,1,0:T(8,128)S(1)}, f32[128,64,64]{2,1,0:T(8,128)}, u32[]{:S(2)}) copy-start(f32[128,64,64]{2,1,0:T(8,128)} %get-tuple-element.213) | copy-start | bytes 6291460 | tf_op jit(solution)/shard_map/while
  303.8 5.5 %copy-start.2 = (f32[128,64,64]{2,1,0:T(8,128)S(1)}, f32[128,64,64]{2,1,0:T(8,128)}, u32[]{:S(2)}) copy-start(f32[128,64,64]{2,1,0:T(8,128)} %get-tuple-element.213) | copy-start | bytes 6291460 | tf_op jit(solution)/shard_map/while
  315.6 5.5 %copy-start.2 = (f32[128,64,64]{2,1,0:T(8,128)S(1)}, f32[128,64,64]{2,1,0:T(8,128)}, u32[]{:S(2)}) copy-start(f32[128,64,64]{2,1,0:T(8,128)} %get-tuple-element.213) | copy-start | bytes 6291460 | tf_op jit(solution)/shard_map/while
  488.1 3.7 copy-start.1
  (10 other events, 18.7 us)
